TPU v7x, 32 devices: a whole 2x2x4 slice. The times are simulated.
32 devices in a mesh: fsdp: 4 (over z), ctx: 2 (over x), tp: 4 (over y, core).
Axes of the slice: x: 2, y: 2, z: 4, core: 2. Of those that a mesh axis runs over, the one named last changes fastest.
Arguments:
- tokens: bfloat16 [4, 2048, 2048], P('fsdp', 'ctx'), may hold values from -6 to 6
- segments: int32 [4, 2048], P('fsdp'), may hold values from 0 to 7, never falling along the last dimension, each value on 1 to 1024 neighbouring positions
- cotangent: bfloat16 [4, 2048, 2048], P('fsdp', 'ctx'), may hold values from -6 to 6
- gain_mix: float32 [2048], replicated, may hold values from 0.5 to 1.5
- w_branch: bfloat16 [2048, 2560], P('fsdp', 'tp'), may hold values from -0.125 to 0.125
- w_input: bfloat16 [2048, 2560], P('fsdp', 'tp'), may hold values from -0.125 to 0.125
- conv_weight: float32 [4, 2560], P(None, 'tp'), may hold values from -3 to 3
- conv_bias: float32 [2560], P('tp'), may hold values from -1.75 to 1.75
- gate_a: bfloat16 [16, 160, 160], P('tp'), may hold values from -0.5 to 0.5
- bias_a: float32 [2560], P('tp'), may hold values from -3 to 3
- gate_x: bfloat16 [16, 160, 160], P('tp'), may hold values from -0.5 to 0.5
- bias_x: float32 [2560], P('tp'), may hold values from -3 to 3
- decay_param: float32 [2560], P('tp'), may hold values from 4 to 8
- w_out: bfloat16 [2560, 2048], P('tp', 'fsdp'), may hold values from -0.3125 to 0.3125
- gain_mlp: float32 [2048], replicated, may hold values from 0.5 to 1.5
- w_gate: bfloat16 [2048, 6144], P('fsdp', 'tp'), may hold values from -0.125 to 0.125
- w_up: bfloat16 [2048, 6144], P('fsdp', 'tp'), may hold values from -0.125 to 0.125
- w_down: bfloat16 [6144, 2048], P('tp', 'fsdp'), may hold values from -0.15625 to 0.15625
Outputs:
- output: bfloat16 [4, 2048, 2048], P('fsdp', 'ctx')
- grad_tokens: bfloat16 [4, 2048, 2048], P('fsdp', 'ctx')
- grad_gain_mix: float32 [2048], replicated
- grad_w_branch: float32 [2048, 2560], P('fsdp', 'tp')
- grad_w_input: float32 [2048, 2560], P('fsdp', 'tp')
- grad_conv_weight: float32 [4, 2560], P(None, 'tp')
- grad_conv_bias: float32 [2560], P('tp')
- grad_gate_a: float32 [16, 160, 160], P('tp')
- grad_bias_a: float32 [2560], P('tp')
- grad_gate_x: float32 [16, 160, 160], P('tp')
- grad_bias_x: float32 [2560], P('tp')
- grad_decay_param: float32 [2560], P('tp')
- grad_w_out: float32 [2560, 2048], P('tp', 'fsdp')
- grad_gain_mlp: float32 [2048], replicated
- grad_w_gate: float32 [2048, 6144], P('fsdp', 'tp')
- grad_w_up: float32 [2048, 6144], P('fsdp', 'tp')
- grad_w_down: float32 [6144, 2048], P('tp', 'fsdp')
Inputs may be any that keep to these rules, and one draw needn't show every extreme that they name: `segments`: within a sequence the document numbers never fall; every document has 1 to 1024 positions and one has exactly 1024.
All inputs are finite; a program needn't handle non-finite values.
Results may differ from a plain program's by a relative error of at most 0.012.
Values may be sent and summed in bfloat16 or wider, within the bound.
A program may use at most 256 MiB of HBM per device.

v0:
```python
import jax
import jax.numpy as jnp
from jax import lax
from jax.sharding import PartitionSpec as P

EPSILON = 1e-06
RATE_SCALE = 8.0


def passed_along(block, axis, distance):
    devices = range(lax.axis_size(axis))
    route = [(i - distance, i) for i in devices if i - distance in devices]
    return lax.ppermute(block, axis, route)


def entering_2(x, axis, combine, identity, reverse):
    length, place = (lax.axis_size(axis), lax.axis_index(axis))
    everything = jax.tree.map(lambda part: lax.all_gather(part, axis), x)
    start = jax.tree.map(
        lambda part, zero: jnp.broadcast_to(jnp.asarray(zero, part.dtype), part.shape), x, identity
    )

    def turn(k, before):
        at = length - 1 - k if reverse else k
        reached = at > place if reverse else at < place
        new = combine(before, jax.tree.map(lambda part: part[at], everything))
        return jax.tree.map(lambda a, b: jnp.where(reached, a, b), new, before)

    return lax.fori_loop(0, length, turn, start)


def linear_combine(earlier, later):
    return (earlier[0] * later[0], later[0] * earlier[1] + later[1])


def matmul(left, right):
    return jnp.dot(left, right, preferred_element_type=jnp.float32)


def left_inner(left, right):
    return lax.dot_general(
        left, right, (((0,), (0,)), ((), ())), preferred_element_type=jnp.float32
    )


def right_inner(left, right):
    return lax.dot_general(
        left, right, (((1,), (1,)), ((), ())), preferred_element_type=jnp.float32
    )


def gelu_slope(values):
    result, pull_back = jax.vjp(lambda inner_v: jax.nn.gelu(inner_v, approximate=True), values)
    return (result, pull_back(jnp.ones_like(values))[0])


def rms_rows(values):
    return lax.rsqrt(jnp.mean(values * values, axis=-1, keepdims=True) + EPSILON)


def norm_back(grad_norm, scaled, scale_row, gain):
    grad_scaled = grad_norm * gain
    return scale_row * (
        grad_scaled - scaled * jnp.mean(grad_scaled * scaled, axis=-1, keepdims=True)
    )


def shards(
    tokens,
    segments,
    cotangent,
    gain_mix,
    w_branch,
    w_input,
    conv_weight,
    conv_bias,
    gate_a,
    bias_a,
    gate_x,
    bias_x,
    decay_param,
    w_out,
    gain_mlp,
    w_gate,
    w_up,
    w_down,
):
    full_branch, full_input, full_gate, full_up, full_out, full_down = (
        lax.all_gather(w_branch, "fsdp", axis=0, tiled=True),
        lax.all_gather(w_input, "fsdp", axis=0, tiled=True),
        lax.all_gather(w_gate, "fsdp", axis=0, tiled=True),
        lax.all_gather(w_up, "fsdp", axis=0, tiled=True),
        lax.all_gather(w_out, "fsdp", axis=1, tiled=True),
        lax.all_gather(w_down, "fsdp", axis=1, tiled=True),
    )
    seq_count, tok_count, model_width = tokens.shape
    row_count = seq_count * tok_count
    kernel = conv_weight.shape[0]
    lag_rows = kernel - 1
    local_width = conv_bias.shape[0]
    head_count = gate_a.shape[0]
    block_width = gate_a.shape[1]
    inputs = tokens.reshape(row_count, model_width).astype(jnp.float32)
    scale_mix = rms_rows(inputs)
    scaled_mix = inputs * scale_mix
    normed = (scaled_mix * gain_mix).astype(jnp.bfloat16)
    branch_pre = matmul(normed, full_branch)
    branch, branch_slope = gelu_slope(branch_pre)
    conv_in = (
        matmul(normed, full_input).astype(jnp.bfloat16).reshape(seq_count, tok_count, local_width)
    )
    first_pos = lax.axis_index("ctx") * tok_count
    padded_seg = jnp.pad(segments, ((0, 0), (lag_rows, lag_rows)), constant_values=-1)
    near_seg = lax.dynamic_slice_in_dim(padded_seg, first_pos, tok_count + 2 * lag_rows, 1)
    own_seg = near_seg[:, lag_rows : lag_rows + tok_count]
    same_back = [
        near_seg[:, lag_rows - offset : lag_rows - offset + tok_count] == own_seg
        for offset in range(kernel)
    ]
    same_ahead = [
        near_seg[:, lag_rows + offset : lag_rows + offset + tok_count] == own_seg
        for offset in range(kernel)
    ]
    tail_rows = passed_along(conv_in[:, tok_count - lag_rows :], "ctx", 1)
    conv_ext = jnp.concatenate([tail_rows, conv_in], axis=1)
    conv_sum = jnp.zeros((seq_count, tok_count, local_width), jnp.float32) + conv_bias
    for offset in range(kernel):
        earlier_in = jnp.where(
            same_back[offset][..., None],
            conv_ext[:, lag_rows - offset : lag_rows - offset + tok_count],
            0.0,
        )
        conv_sum = conv_sum + conv_weight[offset] * earlier_in
    conv_out = conv_sum.astype(jnp.bfloat16)
    conv_heads = conv_out.reshape(seq_count, tok_count, head_count, block_width)
    pre_a = (
        jnp.einsum(
            "sthi,hij->sthj", conv_heads, gate_a, preferred_element_type=jnp.float32
        ).reshape(seq_count, tok_count, local_width)
        + bias_a
    )
    pre_x = (
        jnp.einsum(
            "sthi,hij->sthj", conv_heads, gate_x, preferred_element_type=jnp.float32
        ).reshape(seq_count, tok_count, local_width)
        + bias_x
    )
    recur_gate = jax.nn.sigmoid(pre_a)
    input_gate = jax.nn.sigmoid(pre_x)
    softened = jax.nn.softplus(-decay_param)
    log_decay = -RATE_SCALE * softened * recur_gate
    decay = jnp.exp(log_decay)
    root_term = jnp.sqrt(-jnp.expm1(2.0 * log_decay))
    starts = jnp.logical_not(same_back[1])[..., None]
    multiplier = jnp.where(starts, 1.0, root_term)
    carry_factor = jnp.where(starts, 0.0, decay)
    conv_float = conv_out.astype(jnp.float32)
    driven = input_gate * conv_float * multiplier
    decay_run, local_states = lax.associative_scan(linear_combine, (carry_factor, driven), axis=1)
    ones_state = jnp.ones((seq_count, local_width), jnp.float32)
    zero_state = jnp.zeros((seq_count, local_width), jnp.float32)
    entering = entering_2(
        (decay_run[:, -1], local_states[:, -1]),
        "ctx",
        linear_combine,
        (ones_state, zero_state),
        False,
    )[1]
    states = local_states + decay_run * entering[:, None]
    states_rows = states.reshape(row_count, local_width)
    mixed_out = (states_rows * branch).astype(jnp.bfloat16)
    mixer_term = matmul(mixed_out, full_out)
    resid_rows = inputs + lax.psum(mixer_term, "tp")
    scale_mlp = rms_rows(resid_rows)
    scaled_mlp = resid_rows * scale_mlp
    normed_mlp = (scaled_mlp * gain_mlp).astype(jnp.bfloat16)
    gate_pre = matmul(normed_mlp, full_gate)
    up_pre = matmul(normed_mlp, full_up)
    gate_act, gate_slope = gelu_slope(gate_pre)
    hidden = (gate_act * up_pre).astype(jnp.bfloat16)
    down_term = matmul(hidden, full_down)
    output = (resid_rows + lax.psum(down_term, "tp")).astype(jnp.bfloat16)
    grad_low = cotangent.reshape(row_count, model_width)
    grad_out = grad_low.astype(jnp.float32)
    grad_w_down = left_inner(hidden, grad_low)
    grad_hidden = right_inner(grad_low, full_down)
    grad_gate = (grad_hidden * up_pre * gate_slope).astype(jnp.bfloat16)
    grad_up = (grad_hidden * gate_act).astype(jnp.bfloat16)
    grad_w_gate = left_inner(normed_mlp, grad_gate)
    grad_w_up = left_inner(normed_mlp, grad_up)
    mlp_back_term = right_inner(grad_gate, full_gate) + right_inner(grad_up, full_up)
    grad_norm_mlp = lax.psum(mlp_back_term, "tp")
    grad_resid = grad_out + norm_back(grad_norm_mlp, scaled_mlp, scale_mlp, gain_mlp)
    grad_proj = grad_resid.astype(jnp.bfloat16)
    grad_gain_mlp = jnp.sum(grad_norm_mlp * scaled_mlp, axis=0)
    grad_w_out = left_inner(mixed_out, grad_proj)
    grad_mixed = right_inner(grad_proj, full_out)
    grad_branch = (grad_mixed * states_rows * branch_slope).astype(jnp.bfloat16)
    grad_states = (grad_mixed * branch).reshape(seq_count, tok_count, local_width)
    next_factor = jnp.concatenate(
        [carry_factor[:, 1:], jnp.ones((seq_count, 1, local_width), jnp.float32)], axis=1
    )
    run_back, local_back = lax.associative_scan(
        linear_combine, (jnp.flip(next_factor, 1), jnp.flip(grad_states, 1)), axis=1
    )
    run_back = jnp.flip(run_back, 1)
    local_back = jnp.flip(local_back, 1)
    leaving = (carry_factor[:, 0] * run_back[:, 0], carry_factor[:, 0] * local_back[:, 0])
    arriving = entering_2(leaving, "ctx", linear_combine, (ones_state, zero_state), True)[1]
    grad_total = local_back + run_back * arriving[:, None]
    prev_states = jnp.concatenate([entering[:, None], states[:, :-1]], axis=1)
    grad_mult = grad_total * input_gate * conv_float
    grad_log = jnp.where(
        starts, 0.0, grad_total * prev_states * decay - grad_mult * decay * decay / root_term
    )
    grad_decay_param = (
        RATE_SCALE * jax.nn.sigmoid(-decay_param) * jnp.sum(grad_log * recur_gate, axis=(0, 1))
    )
    grad_pre_a = (grad_log * (-RATE_SCALE * softened) * recur_gate * (1.0 - recur_gate)).astype(
        jnp.bfloat16
    )
    grad_pre_x = (grad_total * conv_float * multiplier * input_gate * (1.0 - input_gate)).astype(
        jnp.bfloat16
    )
    heads_a = grad_pre_a.reshape(seq_count, tok_count, head_count, block_width)
    heads_x = grad_pre_x.reshape(seq_count, tok_count, head_count, block_width)
    grad_gate_a = jnp.einsum(
        "sthi,sthj->hij", conv_heads, heads_a, preferred_element_type=jnp.float32
    )
    grad_gate_x = jnp.einsum(
        "sthi,sthj->hij", conv_heads, heads_x, preferred_element_type=jnp.float32
    )
    grad_bias_a = jnp.sum(grad_pre_a.astype(jnp.float32), axis=(0, 1))
    grad_bias_x = jnp.sum(grad_pre_x.astype(jnp.float32), axis=(0, 1))
    gate_back = jnp.einsum(
        "sthj,hij->sthi", heads_a, gate_a, preferred_element_type=jnp.float32
    ) + jnp.einsum("sthj,hij->sthi", heads_x, gate_x, preferred_element_type=jnp.float32)
    grad_conv = grad_total * input_gate * multiplier + gate_back.reshape(
        seq_count, tok_count, local_width
    )
    head_rows = passed_along(grad_conv[:, :lag_rows], "ctx", -1)
    grad_ext = jnp.concatenate([grad_conv, head_rows], axis=1)
    grad_conv_in = jnp.zeros((seq_count, tok_count, local_width), jnp.float32)
    weight_rows = []
    for offset in range(kernel):
        later_grad = jnp.where(
            same_ahead[offset][..., None], grad_ext[:, offset : offset + tok_count], 0.0
        )
        grad_conv_in = grad_conv_in + conv_weight[offset] * later_grad
        earlier_in = jnp.where(
            same_back[offset][..., None],
            conv_ext[:, lag_rows - offset : lag_rows - offset + tok_count],
            0.0,
        )
        weight_rows.append(jnp.sum(grad_conv * earlier_in, axis=(0, 1)))
    grad_conv_weight = jnp.stack(weight_rows)
    grad_conv_bias = jnp.sum(grad_conv, axis=(0, 1))
    grad_in_low = grad_conv_in.astype(jnp.bfloat16).reshape(row_count, local_width)
    grad_w_input = left_inner(normed, grad_in_low)
    grad_w_branch = left_inner(normed, grad_branch)
    mix_back_term = right_inner(grad_in_low, full_input) + right_inner(grad_branch, full_branch)
    grad_norm_mix = lax.psum(mix_back_term, "tp")
    grad_gain_mix = jnp.sum(grad_norm_mix * scaled_mix, axis=0)
    grad_tokens = (grad_resid + norm_back(grad_norm_mix, scaled_mix, scale_mix, gain_mix)).astype(
        jnp.bfloat16
    )
    owned = (
        lax.psum_scatter(grad_w_branch, "fsdp", scatter_dimension=0, tiled=True),
        lax.psum_scatter(grad_w_input, "fsdp", scatter_dimension=0, tiled=True),
        lax.psum_scatter(grad_w_gate, "fsdp", scatter_dimension=0, tiled=True),
        lax.psum_scatter(grad_w_up, "fsdp", scatter_dimension=0, tiled=True),
        lax.psum_scatter(grad_w_out, "fsdp", scatter_dimension=1, tiled=True),
        lax.psum_scatter(grad_w_down, "fsdp", scatter_dimension=1, tiled=True),
    )
    owned_branch, owned_input, owned_gate, owned_up, owned_out, owned_down = owned
    summed = lax.psum(
        (owned_branch, owned_input, owned_gate, owned_up, owned_out, owned_down), "ctx"
    )
    sum_branch, sum_input, sum_gate, sum_up, sum_out, sum_down = summed
    small_sums = lax.psum(
        (
            grad_gain_mix,
            grad_gain_mlp,
            grad_conv_weight,
            grad_conv_bias,
            grad_gate_a,
            grad_bias_a,
            grad_gate_x,
            grad_bias_x,
            grad_decay_param,
        ),
        ("fsdp", "ctx"),
    )
    (
        sum_gain_mix,
        sum_gain_mlp,
        sum_conv_weight,
        sum_conv_bias,
        sum_gate_a,
        sum_bias_a,
        sum_gate_x,
        sum_bias_x,
        sum_decay,
    ) = small_sums
    return (
        output.reshape(seq_count, tok_count, model_width),
        grad_tokens.reshape(seq_count, tok_count, model_width),
        sum_gain_mix,
        sum_branch,
        sum_input,
        sum_conv_weight,
        sum_conv_bias,
        sum_gate_a,
        sum_bias_a,
        sum_gate_x,
        sum_bias_x,
        sum_decay,
        sum_out,
        sum_gain_mlp,
        sum_gate,
        sum_up,
        sum_down,
    )


def solution(mesh):
    in_specs = (
        P("fsdp", "ctx", None),
        P("fsdp", None),
        P("fsdp", "ctx", None),
        P(),
        P("fsdp", "tp"),
        P("fsdp", "tp"),
        P(None, "tp"),
        P("tp"),
        P("tp", None, None),
        P("tp"),
        P("tp", None, None),
        P("tp"),
        P("tp"),
        P("tp", "fsdp"),
        P(),
        P("fsdp", "tp"),
        P("fsdp", "tp"),
        P("tp", "fsdp"),
    )
    out_specs = (
        P("fsdp", "ctx", None),
        P("fsdp", "ctx", None),
        P(),
        P("fsdp", "tp"),
        P("fsdp", "tp"),
        P(None, "tp"),
        P("tp"),
        P("tp", None, None),
        P("tp"),
        P("tp", None, None),
        P("tp"),
        P("tp"),
        P("tp", "fsdp"),
        P(),
        P("fsdp", "tp"),
        P("fsdp", "tp"),
        P("tp", "fsdp"),
    )
    return jax.shard_map(shards, mesh=mesh, in_specs=in_specs, out_specs=out_specs, check_vma=False)
```

profile of v0, /device:TPU:0, one launch (start us, length us, event | category | flops | bytes accessed | tf_op | source)
XLA Modules:
  0.0 3015.9 jit_solution(510944161602865288)
XLA Ops:
  13.5 53.5 %all-gather.7.cloned.1.call-done = bf16[2048,640]{1,0:T(8,128)(2,1)} async-done(((bf16[512,640]{1,0:T(8,128)(2,1)}), bf16[2048,640]{1,0:T(8,128)(2,1)}) %all-gather.7.cloned.1.call-update) | async-done | bytes 2621456 | tf_op jit(solution)/shard_map/all_gather | solution.py:90
  377.1 12.8 fusion.76
  400.8 150.4 %all-reduce.93.cloned.1.call-done = f32[1024,2048]{1,0:T(8,128)} async-done(((f32[1024,2048]{1,0:T(8,128)}), f32[1024,2048]{1,0:T(8,128)}) %all-reduce.93.cloned.1.call-update) | async-done | bytes 8388624 | tf_op jit(solution)/shard_map/psum | solution.py:173
  563.1 105.0 %all-gather.13.cloned.1.call-done = bf16[2048,1536]{1,0:T(8,128)(2,1)} async-done(((bf16[512,1536]{1,0:T(8,128)(2,1)}), bf16[2048,1536]{1,0:T(8,128)(2,1)}) %all-gather.13.cloned.1.call-update) | async-done | bytes 6291472 | tf_op jit(solution)/shard_map/all_gather | solution.py:91
  668.1 12.2 fusion.139
  680.3 102.8 %all-gather.15.cloned.1.call-done = bf16[2048,1536]{1,0:T(8,128)(2,1)} async-done(((bf16[512,1536]{1,0:T(8,128)(2,1)}), bf16[2048,1536]{1,0:T(8,128)(2,1)}) %all-gather.15.cloned.1.call-update) | async-done | bytes 6291472 | tf_op jit(solution)/shard_map/all_gather | solution.py:92
  794.8 103.4 %all-gather.17.cloned.1.call-done = bf16[1536,2048]{1,0:T(8,128)(2,1)} async-done(((bf16[1536,512]{1,0:T(8,128)(2,1)}), bf16[1536,2048]{1,0:T(8,128)(2,1)}) %all-gather.17.cloned.1.call-update) | async-done | bytes 6291472 | tf_op jit(solution)/shard_map/all_gather | solution.py:94
  898.2 18.2 multiply_convert_fusion.1
  937.2 151.2 %all-reduce.95.cloned.1.call-done = f32[1024,2048]{1,0:T(8,128)} async-done(((f32[1024,2048]{1,0:T(8,128)}), f32[1024,2048]{1,0:T(8,128)}) %all-reduce.95.cloned.1.call-update) | async-done | bytes 8388624 | tf_op jit(solution)/shard_map/psum | solution.py:192
  1166.0 12.5 fusion.54
  1178.4 20.8 reverse.9
  1478.5 20.8 rev.13
  1499.3 20.9 rev.12
  1568.8 12.6 fusion.145
  1581.6 12.5 fusion.146
  1594.1 12.2 fusion.30
  1632.6 29.5 reduce-scatter.9.cloned.1.call-done
  1662.1 214.6 %reduce-scatter.13.cloned.1.call-done = f32[512,1536]{1,0:T(8,128)} async-done(((f32[2048,1536]{1,0:T(8,128)}), f32[512,1536]{1,0:T(8,128)}) %reduce-scatter.13.cloned.1.call-update) | async-done | bytes 3145744 | tf_op jit(solution)/shard_map/reduce_scatter | solution.py:270
  1876.7 215.3 %reduce-scatter.15.cloned.1.call-done = f32[512,1536]{1,0:T(8,128)} async-done(((f32[2048,1536]{1,0:T(8,128)}), f32[512,1536]{1,0:T(8,128)}) %reduce-scatter.15.cloned.1.call-update) | async-done | bytes 3145744 | tf_op jit(solution)/shard_map/reduce_scatter | solution.py:271
  2092.0 215.2 %reduce-scatter.17.cloned.1.call-done = f32[1536,512]{1,0:T(8,128)} async-done(((f32[1536,2048]{1,0:T(8,128)}), f32[1536,512]{1,0:T(8,128)}) %reduce-scatter.17.cloned.1.call-update) | async-done | bytes 3145744 | tf_op jit(solution)/shard_map/reduce_scatter | solution.py:273
  2307.9 291.2 %all-reduce.99.cloned.1.call-done = (f32[1024,2048]{1,0:T(8,128)}, f32[1024,2048]{1,0:T(8,128)}) async-done(((f32[1024,2048]{1,0:T(8,128)}, f32[1024,2048]{1,0:T(8,128)}), (f32[1024,2048]{1,0:T(8,128)}, f32[1024,2048]{1,0:T(8,128)})) %all-reduce.99.cloned.1.call-update) | async-done | bytes 16777232 | tf_op jit(solution)/shard_map/psum | solution.py:182
  2604.9 39.3 %all-reduce.83 = (f32[2048]{0:T(1024)}, f32[4,640]{1,0:T(4,128)}, f32[640]{0:T(1024)}, f32[640]{0:T(1024)}, f32[640]{0:T(1024)}, /*index=5*/f32[640]{0:T(1024)}, f32[2048]{0:T(1024)}) all-reduce(f32[2048]{0:T(1024)S(1)} %get-tuple-element.283, ...), channel_id=1, replica_groups=mesh['fsdp'=4,'ctx'=2,'tp'=4] {'fsdp','ctx'}, use_global_device_ids=true, to_apply=%region_13.14 | all-reduce | flops 9216 | bytes 73728 | tf_op jit(solution)/shard_map/psum | solution.py:280
  2662.3 25.7 all-reduce.97.cloned.1.call-done
  2688.0 307.0 %all-reduce.101.cloned.1.call-done = (f32[512,640]{1,0:T(8,128)}, f32[512,640]{1,0:T(8,128)}, f32[640,512]{1,0:T(8,128)}, f32[512,1536]{1,0:T(8,128)}, f32[512,1536]{1,0:T(8,128)}, /*index=5*/f32[1536,512]{1,0:T(8,128)}) async-done(((f32[512,640]{1,0:T(8,128)}, f32[512,640]{1,0:T(8,128)}, f32[640,512]{1,0:T(8,128)}, f32[512,1536]{1,0:T(8,128)}, f32[512,1536]{1,0:T(8,128)}, ...) | async-done | bytes 13369360 | tf_op jit(solution)/shard_map/psum | solution.py:276
  (728 shorter events, 840.2 us)
Async XLA Ops:
  7.2 79.2 %copy-start = (bf16[4,160,160]{2,1,0:T(8,128)(2,1)S(1)}, bf16[4,160,160]{2,1,0:T(8,128)(2,1)}, u32[]{:S(2)}) copy-start(bf16[4,160,160]{2,1,0:T(8,128)(2,1)} %param.30) | copy-start | bytes 614404
  7.2 59.9 %all-gather.7.cloned.1.call-start = ((), (), s32[]{:S(2)}) async-start(), calls=%async_computation.6 | async-start | bytes 3276800 | tf_op jit(solution)/shard_map/all_gather | solution.py:90
  7.9 369.2 %all-gather.9.cloned.1.call-start = ((), (), s32[]{:S(2)}) async-start(), calls=%async_computation.7 | async-start | bytes 3276800 | tf_op jit(solution)/shard_map/all_gather | solution.py:89
  8.7 381.2 %all-gather.11.cloned.1.call-start = ((), (), s32[]{:S(2)}) async-start(), calls=%async_computation.8 | async-start | bytes 3276800 | tf_op jit(solution)/shard_map/all_gather | solution.py:93
  9.5 541.8 %all-reduce.93.cloned.1.call-start = ((), (), s32[]{:S(2)}) async-start(), calls=%async_computation.9 | async-start | bytes 16777216 | tf_op jit(solution)/shard_map/psum | solution.py:173
  12.7 65.6 %copy-start.76 = (f32[640]{0:T(1024)}, f32[640]{0:T(1024)S(1)}, u32[]{:S(2)}) copy-start(f32[640]{0:T(1024)S(1)} %get-tuple-element.290) | copy-start | bytes 7684
  12.7 65.6 %copy-start.78 = (f32[640]{0:T(1024)}, f32[640]{0:T(1024)S(1)}, u32[]{:S(2)}) copy-start(f32[640]{0:T(1024)S(1)} %get-tuple-element.291) | copy-start | bytes 7684
  12.7 81.2 %copy-start.60 = (f32[640]{0:T(1024)}, f32[640]{0:T(1024)S(1)}, u32[]{:S(2)}) copy-start(f32[640]{0:T(1024)S(1)} %fusion.106) | copy-start | bytes 7684
  73.6 4.7 collective-permute-start
  398.9 269.3 %all-gather.13.cloned.1.call-start = ((), (), s32[]{:S(2)}) async-start(), calls=%async_computation.10 | async-start | bytes 7864320 | tf_op jit(solution)/shard_map/all_gather | solution.py:91
  399.5 383.6 %all-gather.15.cloned.1.call-start = ((), (), s32[]{:S(2)}) async-start(), calls=%async_computation.11 | async-start | bytes 7864320 | tf_op jit(solution)/shard_map/all_gather | solution.py:92
  400.0 498.2 %all-gather.17.cloned.1.call-start = ((), (), s32[]{:S(2)}) async-start(), calls=%async_computation.12 | async-start | bytes 7864320 | tf_op jit(solution)/shard_map/all_gather | solution.py:94
  400.8 159.6 %copy-start.65 = (f32[2048]{0:T(1024)S(1)}, f32[2048]{0:T(1024)}, u32[]{:S(2)}) copy-start(f32[2048]{0:T(1024)} %param.36) | copy-start | bytes 24580
  400.8 687.6 %all-reduce.95.cloned.1.call-start = ((), (), s32[]{:S(2)}) async-start(), calls=%async_computation.13 | async-start | bytes 16777216 | tf_op jit(solution)/shard_map/psum | solution.py:192
  937.2 695.4 %reduce-scatter.11.cloned.1.call-start = ((), (), s32[]{:S(2)}) async-start(), calls=%async_computation.16 | async-start | bytes 6553600 | tf_op jit(solution)/shard_map/reduce_scatter | solution.py:272
  1110.4 522.2 %reduce-scatter.7.cloned.1.call-start = ((), (), s32[]{:S(2)}) async-start(), calls=%async_computation.14 | async-start | bytes 6553600 | tf_op jit(solution)/shard_map/reduce_scatter | solution.py:268
  1342.2 319.9 %reduce-scatter.9.cloned.1.call-start = ((), (), s32[]{:S(2)}) async-start(), calls=%async_computation.15 | async-start | bytes 6553600 | tf_op jit(solution)/shard_map/reduce_scatter | solution.py:269
  1554.1 5.6 collective-permute-start.1
  1568.8 307.9 %reduce-scatter.13.cloned.1.call-start = ((), (), s32[]{:S(2)}) async-start(), calls=%async_computation.17 | async-start | bytes 15728640 | tf_op jit(solution)/shard_map/reduce_scatter | solution.py:270
  1581.5 510.5 %reduce-scatter.15.cloned.1.call-start = ((), (), s32[]{:S(2)}) async-start(), calls=%async_computation.18 | async-start | bytes 15728640 | tf_op jit(solution)/shard_map/reduce_scatter | solution.py:271
  1594.1 713.1 %reduce-scatter.17.cloned.1.call-start = ((), (), s32[]{:S(2)}) async-start(), calls=%async_computation.19 | async-start | bytes 15728640 | tf_op jit(solution)/shard_map/reduce_scatter | solution.py:273
  1606.4 992.6 %all-reduce.99.cloned.1.call-start = ((), (), s32[]{:S(2)}) async-start(), calls=%async_computation.21 | async-start | bytes 33554432 | tf_op jit(solution)/shard_map/psum | solution.py:182
  1627.9 1060.1 %all-reduce.97.cloned.1.call-start = ((), (), s32[]{:S(2)}) async-start(), calls=%async_computation.20 | async-start | bytes 2621440 | tf_op jit(solution)/shard_map/psum | solution.py:280
  1632.5 1362.5 %all-reduce.101.cloned.1.call-start = ((), (), s32[]{:S(2)}) async-start(), calls=%async_computation.22 | async-start | bytes 26738688 | tf_op jit(solution)/shard_map/psum | solution.py:276
  (138 other events, 1560.3 us)
Sparse Core Ops, SparseCore 0:
  9.6 57.4 all-gather.6
  68.6 53.5 all-gather.8
  123.8 53.4 all-gather.10
  399.0 152.1 all-reduce.92
  552.6 115.4 all-gather.12
  669.6 113.5 all-gather.14
  784.7 113.5 all-gather.16
  937.3 151.0 all-reduce.94
  1110.5 93.9 reduce-scatter.10
  1342.3 93.8 reduce-scatter.6
  1568.9 93.1 reduce-scatter.8
  1664.3 212.3 reduce-scatter.12
  1879.1 212.8 reduce-scatter.14
  2094.2 212.8 reduce-scatter.16
  2309.7 289.3 all-reduce.98
  2603.6 84.3 all-reduce.96
  2690.8 304.0 all-reduce.100
where the time goes:
time: 3040 us; the launch traced here: 3020 us
  waiting for transfers between devices  1970 us (65%)
  local copies, waits for them, and re-layouts  565 us (19%)
  other arithmetic  203 us (7%)
  matrix products  194 us (6%)
  blocking collectives  56.9 us (2%)
    psum x1, waiting for transfers between devices, shards(): lax.psum((owned_branch, owned_input, owned_gate, owned_up, owned_out, own...  307 us
    psum x1, waiting for transfers between devices, shards(): output = (resid_rows + lax.psum(down_term, 'tp')).astype(jnp.bfloat16)  291 us
    reduce_scatter x1, waiting for transfers between devices, shards(): lax.psum_scatter(grad_w_up, 'fsdp', scatter_dimension=0, tiled=True)  215 us
    reduce_scatter x1, waiting for transfers between devices, shards(): lax.psum_scatter(grad_w_down, 'fsdp', scatter_dimension=1, tiled=True)  215 us
    reduce_scatter x1, waiting for transfers between devices, shards(): lax.psum_scatter(grad_w_gate, 'fsdp', scatter_dimension=0, tiled=True)  215 us
    slice x70, local copies, waits for them, and re-layouts, shards(): lax.associative_scan(linear_combine, (jnp.flip(next_factor, 1), jnp.flip(...  170 us
    psum x1, waiting for transfers between devices, shards(): grad_norm_mlp = lax.psum(mlp_back_term, 'tp')  151 us
    psum x1, waiting for transfers between devices, shards(): resid_rows = inputs + lax.psum(mixer_term, 'tp')  150 us
  transfers between devices with their start and end apart: 19, of which 15 were waited for; matrix products, arithmetic and copies ran while one was open for 29% of the time, Pallas kernels for 0%

commit v1 on v0

--- a/solution.py
+++ b/solution.py
@@ -5,6 +5,28 @@
 
 EPSILON = 1e-06
 RATE_SCALE = 8.0
+
+
+def laid_out(pieces, dim):
+    shape = list(pieces.shape[1:])
+    shape[dim] *= pieces.shape[0]
+    return jnp.moveaxis(pieces, 0, dim).reshape(shape)
+
+
+def collect(shard, axis, dim):
+    peers = lax.axis_size(axis)
+    pairs = [(i, (i + 1) % peers) for i in range(peers)]
+    back = [(b, a) for a, b in pairs]
+    lower, upper = ([], [])
+    for turn in range(peers - 1):
+        if turn % 2 == 0:
+            lower.append(lax.ppermute(lower[-1] if lower else shard, axis, pairs))
+        else:
+            upper.append(lax.ppermute(upper[-1] if upper else shard, axis, back))
+    parts = jnp.stack([*lower[::-1], shard, *upper])
+    shift = lax.axis_index(axis) - len(lower)
+    parts = parts[(jnp.arange(peers) - shift) % peers]
+    return laid_out(parts, dim)
 
 
 def passed_along(block, axis, distance):
@@ -91,7 +113,7 @@
         lax.all_gather(w_gate, "fsdp", axis=0, tiled=True),
         lax.all_gather(w_up, "fsdp", axis=0, tiled=True),
         lax.all_gather(w_out, "fsdp", axis=1, tiled=True),
-        lax.all_gather(w_down, "fsdp", axis=1, tiled=True),
+        collect(w_down, "fsdp", 1),
     )
     seq_count, tok_count, model_width = tokens.shape
     row_count = seq_count * tok_count

time: 3040 us -> 2870 us (0.944)
  waiting for transfers between devices: 1970 us -> 1820 us
  starting transfers between devices: 5.35 us -> 36.9 us
    psum x1, waiting for transfers between devices: 150 us -> 28.2 us  [shards(): resid_rows = inputs + lax.psum(mixer_term, 'tp')]
    all_gather x1 -> x0, waiting for transfers between devices: 103 us -> none  [shards(): lax.all_gather(w_down, 'fsdp', axis=1, tiled=True)]
    ppermute x0 -> x3, waiting for transfers between devices: none -> 70.7 us  [the longest x2 68.3 us: collect(): lower.append(lax.ppermute(lower[-1] if lower else shard, axis, pairs))]
    pad x36, local copies, waits for them, and re-layouts: 76.9 us -> 34.2 us  [shards(): lax.associative_scan(linear_combine, (carry_factor, driven), axis=1)]
    ppermute x0 -> x3, starting transfers between devices: none -> 31.6 us  [the longest x2 27.7 us: collect(): lower.append(lax.ppermute(lower[-1] if lower else shard, axis, pairs))]
  transfers between devices with their start and end apart: 19 -> 21, of which waited for: 15 -> 17; matrix products, arithmetic and copies ran while one was open for 29% -> 29% of each run, Pallas kernels for 0% -> 0%
where the time goes in v1:
time: 2870 us; the launch traced here: 2850 us
  waiting for transfers between devices  1820 us (63%)
  local copies, waits for them, and re-layouts  540 us (19%)
  other arithmetic  191 us (7%)
  matrix products  190 us (7%)
  blocking collectives  56.9 us (2%)
  starting transfers between devices  36.9 us (1%)
    psum x1, waiting for transfers between devices, shards(): lax.psum((owned_branch, owned_input, owned_gate, owned_up, owned_out, own...  307 us
    psum x1, waiting for transfers between devices, shards(): output = (resid_rows + lax.psum(down_term, 'tp')).astype(jnp.bfloat16)  291 us
    reduce_scatter x1, waiting for transfers between devices, shards(): lax.psum_scatter(grad_w_down, 'fsdp', scatter_dimension=1, tiled=True)  215 us
    reduce_scatter x1, waiting for transfers between devices, shards(): lax.psum_scatter(grad_w_up, 'fsdp', scatter_dimension=0, tiled=True)  215 us
    reduce_scatter x1, waiting for transfers between devices, shards(): lax.psum_scatter(grad_w_gate, 'fsdp', scatter_dimension=0, tiled=True)  215 us
    slice x70, local copies, waits for them, and re-layouts, shards(): lax.associative_scan(linear_combine, (jnp.flip(next_factor, 1), jnp.flip(...  171 us
    psum x1, waiting for transfers between devices, shards(): grad_norm_mlp = lax.psum(mlp_back_term, 'tp')  151 us
    slice x68, local copies, waits for them, and re-layouts, shards(): lax.associative_scan(linear_combine, (carry_factor, driven), axis=1)  130 us
  transfers between devices with their start and end apart: 21, of which 17 were waited for; matrix products, arithmetic and copies ran while one was open for 29% of the time, Pallas kernels for 0%

profile of v1, /device:TPU:0, one launch (start us, length us, event | category | flops | bytes accessed | tf_op | source)
XLA Modules:
  0.0 2849.6 jit_solution(7622508120511195051)
XLA Ops:
  13.5 53.5 %all-gather.6.cloned.1.call-done = bf16[2048,640]{1,0:T(8,128)(2,1)} async-done(((bf16[512,640]{1,0:T(8,128)(2,1)}), bf16[2048,640]{1,0:T(8,128)(2,1)}) %all-gather.6.cloned.1.call-update) | async-done | bytes 2621456 | tf_op jit(solution)/shard_map/all_gather | solution.py:112
  316.4 12.4 fusion.77
  341.9 35.2 %collective-permute-done.1 = bf16[1536,512]{1,0:T(8,128)(2,1)S(1)} collective-permute-done((bf16[1536,512]{1,0:T(8,128)(2,1)S(1)}, bf16[1536,512]{1,0:T(8,128)(2,1)S(1)}, u32[]{:S(2)}, u32[]{:S(2)}) %collective-permute-start.1) | collective-permute-done | bytes 1572896 | tf_op jit(solution)/shard_map/ppermute | solution.py:23
  377.1 27.7 collective-permute-start.2
  407.3 33.0 %collective-permute-done.2 = bf16[1536,512]{1,0:T(8,128)(2,1)} collective-permute-done((bf16[1536,512]{1,0:T(8,128)(2,1)S(1)}, bf16[1536,512]{1,0:T(8,128)(2,1)}, u32[]{:S(2)}, u32[]{:S(2)}) %collective-permute-start.2) | collective-permute-done | bytes 1572896 | tf_op jit(solution)/shard_map/ppermute | solution.py:23
  460.8 28.2 all-reduce.93.cloned.1.call-done
  500.9 105.0 %all-gather.12.cloned.1.call-done = bf16[2048,1536]{1,0:T(8,128)(2,1)} async-done(((bf16[512,1536]{1,0:T(8,128)(2,1)}), bf16[2048,1536]{1,0:T(8,128)(2,1)}) %all-gather.12.cloned.1.call-update) | async-done | bytes 6291472 | tf_op jit(solution)/shard_map/all_gather | solution.py:113
  617.7 103.3 %all-gather.14.cloned.1.call-done = bf16[2048,1536]{1,0:T(8,128)(2,1)} async-done(((bf16[512,1536]{1,0:T(8,128)(2,1)}), bf16[2048,1536]{1,0:T(8,128)(2,1)}) %all-gather.14.cloned.1.call-update) | async-done | bytes 6291472 | tf_op jit(solution)/shard_map/all_gather | solution.py:114
  732.8 15.8 fusion.25
  769.0 151.1 %all-reduce.95.cloned.1.call-done = f32[1024,2048]{1,0:T(8,128)} async-done(((f32[1024,2048]{1,0:T(8,128)}), f32[1024,2048]{1,0:T(8,128)}) %all-reduce.95.cloned.1.call-update) | async-done | bytes 8388624 | tf_op jit(solution)/shard_map/psum | solution.py:214
  999.8 12.3 fusion.55
  1012.1 20.8 reverse.9
  1311.6 20.8 rev.13
  1332.4 21.0 rev.12
  1402.3 12.9 fusion.148
  1415.3 12.5 fusion.149
  1466.3 29.3 %reduce-scatter.9.cloned.1.call-done = f32[512,640]{1,0:T(8,128)} async-done(((f32[2048,640]{1,0:T(8,128)}), f32[512,640]{1,0:T(8,128)}) %reduce-scatter.9.cloned.1.call-update) | async-done | bytes 1310736 | tf_op jit(solution)/shard_map/reduce_scatter | solution.py:291
  1495.6 214.8 %reduce-scatter.13.cloned.1.call-done = f32[512,1536]{1,0:T(8,128)} async-done(((f32[2048,1536]{1,0:T(8,128)}), f32[512,1536]{1,0:T(8,128)}) %reduce-scatter.13.cloned.1.call-update) | async-done | bytes 3145744 | tf_op jit(solution)/shard_map/reduce_scatter | solution.py:292
  1710.4 215.2 %reduce-scatter.15.cloned.1.call-done = f32[512,1536]{1,0:T(8,128)} async-done(((f32[2048,1536]{1,0:T(8,128)}), f32[512,1536]{1,0:T(8,128)}) %reduce-scatter.15.cloned.1.call-update) | async-done | bytes 3145744 | tf_op jit(solution)/shard_map/reduce_scatter | solution.py:293
  1925.6 215.3 %reduce-scatter.17.cloned.1.call-done = f32[1536,512]{1,0:T(8,128)} async-done(((f32[1536,2048]{1,0:T(8,128)}), f32[1536,512]{1,0:T(8,128)}) %reduce-scatter.17.cloned.1.call-update) | async-done | bytes 3145744 | tf_op jit(solution)/shard_map/reduce_scatter | solution.py:295
  2141.6 291.2 %all-reduce.99.cloned.1.call-done = (f32[1024,2048]{1,0:T(8,128)}, f32[1024,2048]{1,0:T(8,128)}) async-done(((f32[1024,2048]{1,0:T(8,128)}, f32[1024,2048]{1,0:T(8,128)}), (f32[1024,2048]{1,0:T(8,128)}, f32[1024,2048]{1,0:T(8,128)})) %all-reduce.99.cloned.1.call-update) | async-done | bytes 16777232 | tf_op jit(solution)/shard_map/psum | solution.py:204
  2438.6 39.3 %all-reduce.83 = (f32[2048]{0:T(1024)}, f32[4,640]{1,0:T(4,128)}, f32[640]{0:T(1024)}, f32[640]{0:T(1024)}, f32[640]{0:T(1024)}, /*index=5*/f32[640]{0:T(1024)}, f32[2048]{0:T(1024)}) all-reduce(f32[2048]{0:T(1024)S(1)} %get-tuple-element.283, ...), channel_id=1, replica_groups=mesh['fsdp'=4,'ctx'=2,'tp'=4] {'fsdp','ctx'}, use_global_device_ids=true, to_apply=%region_13.14 | all-reduce | flops 9216 | bytes 73728 | tf_op jit(solution)/shard_map/psum | solution.py:302
  2496.0 25.7 all-reduce.97.cloned.1.call-done
  2521.7 307.0 %all-reduce.101.cloned.1.call-done = (f32[512,640]{1,0:T(8,128)}, f32[512,640]{1,0:T(8,128)}, f32[640,512]{1,0:T(8,128)}, f32[512,1536]{1,0:T(8,128)}, f32[512,1536]{1,0:T(8,128)}, /*index=5*/f32[1536,512]{1,0:T(8,128)}) async-done(((f32[512,640]{1,0:T(8,128)}, f32[512,640]{1,0:T(8,128)}, f32[640,512]{1,0:T(8,128)}, f32[512,1536]{1,0:T(8,128)}, f32[512,1536]{1,0:T(8,128)}, ...) | async-done | bytes 13369360 | tf_op jit(solution)/shard_map/psum | solution.py:298
  (725 shorter events, 830.0 us)
Async XLA Ops:
  7.2 79.0 %copy-start = (bf16[4,160,160]{2,1,0:T(8,128)(2,1)S(1)}, bf16[4,160,160]{2,1,0:T(8,128)(2,1)}, u32[]{:S(2)}) copy-start(bf16[4,160,160]{2,1,0:T(8,128)(2,1)} %param.30) | copy-start | bytes 614404
  7.2 59.9 %all-gather.6.cloned.1.call-start = ((), (), s32[]{:S(2)}) async-start(), calls=%async_computation.6 | async-start | bytes 3276800 | tf_op jit(solution)/shard_map/all_gather | solution.py:112
  7.9 308.4 %all-gather.8.cloned.1.call-start = ((), (), s32[]{:S(2)}) async-start(), calls=%async_computation.7 | async-start | bytes 3276800 | tf_op jit(solution)/shard_map/all_gather | solution.py:111
  8.7 320.1 %all-gather.10.cloned.1.call-start = ((), (), s32[]{:S(2)}) async-start(), calls=%async_computation.8 | async-start | bytes 3276800 | tf_op jit(solution)/shard_map/all_gather | solution.py:115
  9.5 479.6 %all-reduce.93.cloned.1.call-start = ((), (), s32[]{:S(2)}) async-start(), calls=%async_computation.9 | async-start | bytes 16777216 | tf_op jit(solution)/shard_map/psum | solution.py:195
  12.7 65.6 %copy-start.73 = (f32[640]{0:T(1024)}, f32[640]{0:T(1024)S(1)}, u32[]{:S(2)}) copy-start(f32[640]{0:T(1024)S(1)} %get-tuple-element.290) | copy-start | bytes 7684
  12.7 81.1 %copy-start.61 = (f32[640]{0:T(1024)}, f32[640]{0:T(1024)S(1)}, u32[]{:S(2)}) copy-start(f32[640]{0:T(1024)S(1)} %fusion.107) | copy-start | bytes 7684
  73.6 4.7 collective-permute-start
  336.7 269.3 %all-gather.12.cloned.1.call-start = ((), (), s32[]{:S(2)}) async-start(), calls=%async_computation.10 | async-start | bytes 7864320 | tf_op jit(solution)/shard_map/all_gather | solution.py:113
  337.3 383.7 %all-gather.14.cloned.1.call-start = ((), (), s32[]{:S(2)}) async-start(), calls=%async_computation.11 | async-start | bytes 7864320 | tf_op jit(solution)/shard_map/all_gather | solution.py:114
  337.8 582.3 %all-reduce.95.cloned.1.call-start = ((), (), s32[]{:S(2)}) async-start(), calls=%async_computation.12 | async-start | bytes 16777216 | tf_op jit(solution)/shard_map/psum | solution.py:214
  338.1 39.1 %collective-permute-start.1 = (bf16[1536,512]{1,0:T(8,128)(2,1)S(1)}, bf16[1536,512]{1,0:T(8,128)(2,1)S(1)}, u32[]{:S(2)}, u32[]{:S(2)}) collective-permute-start(bf16[1536,512]{1,0:T(8,128)(2,1)S(1)} %copy-done.42), channel_id=1, source_target_pairs={{0,8},{8,16},{16,24},{24,0},{1,9},{9,17},{17,25},{25,1},{2,10},{10... | collective-permute-start | bytes 4718600 | tf_op jit(solution)/shard_map/ppermute | solution.py:23
  338.1 69.2 %collective-permute-start.3 = (bf16[1536,512]{1,0:T(8,128)(2,1)S(1)}, bf16[1536,512]{1,0:T(8,128)(2,1)}, u32[]{:S(2)}, u32[]{:S(2)}) collective-permute-start(bf16[1536,512]{1,0:T(8,128)(2,1)S(1)} %copy-done.42), channel_id=1, source_target_pairs={{8,0},{16,8},{24,16},{0,24},{9,1},{17,9},{25,17},{1,25},{10,2},{18... | collective-permute-start | bytes 4718600 | tf_op jit(solution)/shard_map/ppermute | solution.py:25
  377.1 63.2 %collective-permute-start.2 = (bf16[1536,512]{1,0:T(8,128)(2,1)S(1)}, bf16[1536,512]{1,0:T(8,128)(2,1)}, u32[]{:S(2)}, u32[]{:S(2)}) collective-permute-start(bf16[1536,512]{1,0:T(8,128)(2,1)S(1)} %collective-permute-done.1), channel_id=1, source_target_pairs={{0,8},{8,16},{16,24},{24,0},{1,9},{9,17},{17,25},{25,1},{2,10},{10... | collective-permute-start | bytes 4718600 | tf_op jit(solution)/shard_map/ppermute | solution.py:23
  768.9 697.3 %reduce-scatter.11.cloned.1.call-start = ((), (), s32[]{:S(2)}) async-start(), calls=%async_computation.15 | async-start | bytes 6553600 | tf_op jit(solution)/shard_map/reduce_scatter | solution.py:294
  942.1 524.2 %reduce-scatter.7.cloned.1.call-start = ((), (), s32[]{:S(2)}) async-start(), calls=%async_computation.13 | async-start | bytes 6553600 | tf_op jit(solution)/shard_map/reduce_scatter | solution.py:290
  1175.9 319.7 %reduce-scatter.9.cloned.1.call-start = ((), (), s32[]{:S(2)}) async-start(), calls=%async_computation.14 | async-start | bytes 6553600 | tf_op jit(solution)/shard_map/reduce_scatter | solution.py:291
  1387.5 5.6 collective-permute-start.4
  1402.2 308.2 %reduce-scatter.13.cloned.1.call-start = ((), (), s32[]{:S(2)}) async-start(), calls=%async_computation.16 | async-start | bytes 15728640 | tf_op jit(solution)/shard_map/reduce_scatter | solution.py:292
  1415.2 510.4 %reduce-scatter.15.cloned.1.call-start = ((), (), s32[]{:S(2)}) async-start(), calls=%async_computation.17 | async-start | bytes 15728640 | tf_op jit(solution)/shard_map/reduce_scatter | solution.py:293
  1427.8 713.1 %reduce-scatter.17.cloned.1.call-start = ((), (), s32[]{:S(2)}) async-start(), calls=%async_computation.18 | async-start | bytes 15728640 | tf_op jit(solution)/shard_map/reduce_scatter | solution.py:295
  1440.1 992.6 %all-reduce.99.cloned.1.call-start = ((), (), s32[]{:S(2)}) async-start(), calls=%async_computation.20 | async-start | bytes 33554432 | tf_op jit(solution)/shard_map/psum | solution.py:204
  1461.6 1060.1 %all-reduce.97.cloned.1.call-start = ((), (), s32[]{:S(2)}) async-start(), calls=%async_computation.19 | async-start | bytes 2621440 | tf_op jit(solution)/shard_map/psum | solution.py:302
  1466.2 1362.5 %all-reduce.101.cloned.1.call-start = ((), (), s32[]{:S(2)}) async-start(), calls=%async_computation.21 | async-start | bytes 26738688 | tf_op jit(solution)/shard_map/psum | solution.py:298
  (134 other events, 1504.3 us)
Sparse Core Ops, SparseCore 0:
  9.6 57.4 all-gather.5
  68.6 53.5 all-gather.7
  123.8 53.4 all-gather.9
  336.8 152.2 all-reduce.92
  490.5 115.4 all-gather.11
  607.4 113.5 all-gather.13
  769.1 151.0 all-reduce.94
  942.2 93.9 reduce-scatter.10
  1176.0 93.9 reduce-scatter.6
  1402.4 93.2 reduce-scatter.8
  1498.0 212.3 reduce-scatter.12
  1712.6 212.8 reduce-scatter.14
  1927.9 212.8 reduce-scatter.16
  2143.4 289.3 all-reduce.98
  2437.4 84.3 all-reduce.96
  2524.6 304.0 all-reduce.100
